TPU v7x, 512 devices: a whole 4x4x16 slice. The times are simulated.
512 devices in a mesh: dp: 128 (over z, y, core), shard: 4 (over x).
Axes of the slice: x: 4, y: 4, z: 16, core: 2. Of those that a mesh axis runs over, the one named last changes fastest.
Arguments:
- key_grad: bfloat16 [128, 512, 2560], P('dp', 'shard'), may hold values from -90 to 90
- key_error: float32 [128, 512, 2560], P('dp', 'shard'), may hold values from -4 to 4
- router_grad: bfloat16 [128, 64, 2560], P('dp', 'shard'), may hold values from -90 to 90
- router_error: float32 [128, 64, 2560], P('dp', 'shard'), may hold values from -4 to 4
- norm_grad: bfloat16 [128, 2, 2560], P('dp', None, 'shard'), may hold values from -8 to 8
- key_basis: float32 [32, 2560], replicated, may hold values from -6 to 6
- router_basis: float32 [32, 2560], replicated, may hold values from -6 to 6
- key_momentum: float32 [512, 2560], P('shard', 'dp'), may hold values from -4 to 4
- key_weight: float32 [512, 2560], P('shard', 'dp'), may hold values from -4 to 4
- router_momentum: float32 [64, 2560], P('shard', 'dp'), may hold values from -4 to 4
- router_weight: float32 [64, 2560], P('shard', 'dp'), may hold values from -4 to 4
- norm_momentum: float32 [2, 2560], P(None, 'shard'), may hold values from -4 to 4
- norm_weight: float32 [2, 2560], P(None, 'shard'), may hold values from 0.5 to 1.5
Outputs:
- key_carry: float32 [128, 512, 2560], P('dp', 'shard')
- router_carry: float32 [128, 64, 2560], P('dp', 'shard')
- key_velocity: float32 [512, 2560], P('shard', 'dp')
- key_master: float32 [512, 2560], P('shard', 'dp')
- key_params: bfloat16 [512, 2560], P(None, 'dp')
- router_velocity: float32 [64, 2560], P('shard', 'dp')
- router_master: float32 [64, 2560], P('shard', 'dp')
- router_params: bfloat16 [64, 2560], P(None, 'dp')
- norm_velocity: float32 [2, 2560], P(None, 'shard')
- norm_master: float32 [2, 2560], P(None, 'shard')
- norm_params: bfloat16 [2, 2560], replicated
All inputs are finite; a program needn't handle non-finite values.
Results may differ from a plain program's by a relative error of at most 0.008.
Values may be sent and summed in bfloat16 or wider, within the bound.
No kernel may reach another device: no remote copies, remote signals or barrier semaphores. Data moves between devices by JAX's collectives and lax.ppermute only.
A program may use at most 64 MiB of HBM per device.

v0:
```python
import jax
import jax.numpy as jnp
from jax import lax
from jax.sharding import PartitionSpec as P

ROOT_STEPS = 4
highest = lax.Precision.HIGHEST
momentum_decay = 0.9
learning_rate = 0.1


def inverse_root(gram_matrix):
    scaling = jnp.sqrt(jnp.sum(gram_matrix * gram_matrix)) + 1e-06
    identity = jnp.eye(gram_matrix.shape[0], dtype=jnp.float32)
    square_side = gram_matrix / scaling
    root_side = identity
    for sweep_index in range(ROOT_STEPS):
        middle = 1.5 * identity - 0.5 * jnp.dot(root_side, square_side, precision=highest)
        square_side = jnp.dot(square_side, middle, precision=highest)
        root_side = jnp.dot(middle, root_side, precision=highest)
    return (root_side, scaling)


def project(old_basis, merged):
    return lax.dot_general(old_basis, merged, (((1,), (1,)), ((), ())), precision=highest)


def gram_of(factor_rows):
    return lax.dot_general(factor_rows, factor_rows, (((1,), (1,)), ((), ())), precision=highest)


def normalize(gram_matrix, factor_rows):
    root_side, scaling = inverse_root(gram_matrix)
    return jnp.dot(root_side, factor_rows, precision=highest) / jnp.sqrt(scaling)


def advance(momentum, weight, direction):
    velocity = momentum_decay * momentum + direction
    return (velocity, weight - learning_rate * velocity)


def body(
    key_grad,
    key_error,
    router_grad,
    router_error,
    norm_grad,
    key_basis,
    router_basis,
    key_momentum,
    key_weight,
    router_momentum,
    router_weight,
    norm_momentum,
    norm_weight,
):
    replicas = lax.axis_size("dp")
    rank_size = key_basis.shape[0]
    merged_key = key_grad[0].astype(jnp.float32) + key_error[0]
    merged_router = router_grad[0].astype(jnp.float32) + router_error[0]
    rows_key, rows_router, norm_sum = lax.psum(
        (
            project(key_basis, merged_key),
            project(router_basis, merged_router),
            norm_grad[0].astype(jnp.float32),
        ),
        "dp",
    )
    gram_key, gram_router = lax.psum((gram_of(rows_key), gram_of(rows_router)), "shard")
    ortho_key = normalize(gram_key, rows_key)
    ortho_router = normalize(gram_router, rows_router)
    key_part = lax.dot_general(merged_key, ortho_key, (((0,), (1,)), ((), ())), precision=highest)
    router_part = lax.dot_general(
        merged_router, ortho_router, (((0,), (1,)), ((), ())), precision=highest
    )
    column_sum = lax.psum(jnp.concatenate([key_part, router_part], axis=1), ("dp", "shard"))
    columns = column_sum / replicas
    approx_key = lax.dot_general(
        ortho_key, columns[:, :rank_size], (((0,), (1,)), ((), ())), precision=highest
    )
    approx_router = lax.dot_general(
        ortho_router, columns[:, rank_size:], (((0,), (1,)), ((), ())), precision=highest
    )
    col_width = key_momentum.shape[1]
    offset = lax.axis_index("dp") * col_width
    key_velocity, key_master = advance(
        key_momentum, key_weight, lax.dynamic_slice_in_dim(approx_key, offset, col_width, 1)
    )
    router_velocity, router_master = advance(
        router_momentum,
        router_weight,
        lax.dynamic_slice_in_dim(approx_router, offset, col_width, 1),
    )
    norm_velocity, norm_master = advance(norm_momentum, norm_weight, norm_sum / replicas)
    key_params, router_params, norm_params = (
        lax.all_gather(key_master.astype(jnp.bfloat16), "shard", axis=0, tiled=True),
        lax.all_gather(router_master.astype(jnp.bfloat16), "shard", axis=0, tiled=True),
        lax.all_gather(norm_master.astype(jnp.bfloat16), "shard", axis=1, tiled=True),
    )
    key_carry = (merged_key - approx_key)[None]
    router_carry = (merged_router - approx_router)[None]
    return (
        key_carry,
        router_carry,
        key_velocity,
        key_master,
        key_params,
        router_velocity,
        router_master,
        router_params,
        norm_velocity,
        norm_master,
        norm_params,
    )


def solution(mesh):
    return jax.shard_map(
        body,
        mesh=mesh,
        in_specs=(
            P("dp", "shard", None),
            P("dp", "shard", None),
            P("dp", "shard", None),
            P("dp", "shard", None),
            P("dp", None, "shard"),
            P(),
            P(),
            P("shard", "dp"),
            P("shard", "dp"),
            P("shard", "dp"),
            P("shard", "dp"),
            P(None, "shard"),
            P(None, "shard"),
        ),
        out_specs=(
            P("dp", "shard", None),
            P("dp", "shard", None),
            P("shard", "dp"),
            P("shard", "dp"),
            P(None, "dp"),
            P("shard", "dp"),
            P("shard", "dp"),
            P(None, "dp"),
            P(None, "shard"),
            P(None, "shard"),
            P(),
        ),
        check_vma=False,
    )
```

profile of v0, /device:TPU:8, one launch (start us, length us, event | category | flops | bytes accessed | tf_op | source)
XLA Modules:
  0.0 1036.4 jit_solution(1657459035492836335)
XLA Ops:
  7.2 0.0 copy-start
  7.2 0.0 all-reduce.4.cloned.1.call-start
  7.2 0.7 bitcast_convert_fusion
  8.0 1.4 convolution_bitcast_fusion
  9.4 0.0 copy-done
  9.5 0.0 copy-start.2
  9.5 2.9 fusion.5
  12.4 497.1 %all-reduce = (f32[32,128]{1,0:T(8,128)S(1)}, f32[32,16]{0,1:T(8,128)S(1)}, f32[2,640]{1,0:T(2,128)S(1)}) all-reduce(f32[32,128]{1,0:T(8,128)S(1)} %fusion.5, f32[32,16]{0,1:T(8,128)S(1)} %convolution_bitcast_fusion, f32[2,640]{1,0:T(2,128)S(1)} %bitcast_convert_fusion), channel_id=1, replica_groups=mesh['dp'=128,'shard'=4] {'dp'}, use_global_device_ids=true, to_apply=%region_0.0 | all-reduce | flops 5888 | bytes 47104 | tf_op jit(solution)/shard_map/psum | solution.py:61
  509.5 0.1 fusion.31
  509.6 0.2 fusion.37
  509.9 17.1 %all-reduce.1 = (f32[32,32]{1,0:T(8,128)S(1)}, f32[32,32]{1,0:T(8,128)S(1)}) all-reduce(f32[32,32]{1,0:T(8,128)S(1)} %fusion.31, f32[32,32]{1,0:T(8,128)S(1)} %fusion.37), channel_id=1, replica_groups=mesh['dp'=128,'shard'=4] {'shard'}, use_global_device_ids=true, to_apply=%region_1.0 | all-reduce | flops 2048 | bytes 16384 | tf_op jit(solution)/shard_map/psum | solution.py:69
  527.0 0.6 multiply_reduce_fusion
  528.3 0.1 fusion.11
  528.4 0.1 fusion.27
  528.6 0.1 fusion.24
  528.7 0.2 fusion.10
  528.9 0.1 fusion.39
  529.0 0.1 fusion.38
  529.2 0.2 fusion.9
  529.3 0.1 fusion.40
  529.5 0.1 fusion.41
  530.4 0.1 fusion.15
  530.5 0.1 fusion.26
  530.7 0.1 fusion.25
  530.8 0.2 fusion.14
  531.0 0.1 fusion.33
  531.1 0.1 fusion.32
  531.3 0.2 fusion.13
  531.4 0.1 fusion.34
  531.6 0.0 copy-start.3
  531.6 0.0 copy-start.4
  531.6 0.1 fusion.35
  531.7 0.2 fusion.8
  531.9 0.1 fusion.42
  532.0 0.2 fusion.12
  532.2 0.1 fusion.36
  532.3 0.2 convolution_divide_fusion
  532.5 0.9 fusion
  533.5 0.1 convolution_divide_fusion.1
  533.6 0.0 copy-done.3
  533.6 0.0 copy-start.5
  533.6 0.5 fusion.20
  534.1 0.9 pad_maximum_fusion
  535.0 0.0 all-reduce.4.cloned.1.call-update
  535.0 0.6 fusion.28
  535.6 11.8 %all_gather.11 = bf16[2,2560]{1,0:T(2,128)(2,1)S(1)} all-gather(bf16[2,640]{1,0:T(2,128)(2,1)S(1)} %get-tuple-element.27), channel_id=1, replica_groups=mesh['dp'=128,'shard'=4] {'shard'}, dimensions={1}, use_global_device_ids=true | all-gather | bytes 12800 | tf_op jit(solution)/shard_map/all_gather | solution.py:98
  547.4 0.1 copy.24
  547.5 0.1 copy.25
  547.6 445.8 %all-reduce.4.cloned.1.call-done = f32[2560,64]{0,1:T(8,128)} async-done(((f32[2560,64]{0,1:T(8,128)}), f32[2560,64]{0,1:T(8,128)}) %all-reduce.4.cloned.1.call-update) | async-done | bytes 655376 | tf_op jit(solution)/shard_map/psum | solution.py:76
  993.4 1.1 broadcast_multiply_fusion
  994.6 0.0 copy-start.7
  994.6 0.3 fusion.16
  994.9 2.3 fusion.18
  997.2 0.7 fusion.23
  997.9 0.7 fusion.29
  998.6 12.0 %all_gather.10 = bf16[64,20]{1,0:T(8,128)(2,1)S(1)} all-gather(bf16[16,20]{1,0:T(8,128)(2,1)S(1)} %get-tuple-element.30), channel_id=1, replica_groups=mesh['dp'=128,'shard'=4] {'shard'}, dimensions={0}, use_global_device_ids=true | all-gather | bytes 3200 | tf_op jit(solution)/shard_map/all_gather | solution.py:97
  1010.6 0.7 copy.29
  1011.3 2.6 fusion.4
  1013.9 1.0 fusion.30
  1014.8 0.7 copy.27
  1015.5 0.7 copy.26
  1016.2 12.0 %all_gather.9 = bf16[512,20]{1,0:T(8,128)(2,1)S(1)} all-gather(bf16[128,20]{1,0:T(8,128)(2,1)S(1)} %get-tuple-element.33), channel_id=1, replica_groups=mesh['dp'=128,'shard'=4] {'shard'}, dimensions={0}, use_global_device_ids=true | all-gather | bytes 25600 | tf_op jit(solution)/shard_map/all_gather | solution.py:96
  1028.2 0.7 copy.28
  1028.9 0.6 copy.32
  (14 shorter events, 0.0 us)
Async XLA Ops:
  7.2 2.3 copy-start
  7.2 986.2 %all-reduce.4.cloned.1.call-start = ((), (), s32[]{:S(2)}) async-start(), calls=%async_computation | async-start | bytes 1310720 | tf_op jit(solution)/shard_map/psum | solution.py:76
  9.4 523.1 %copy-start.1 = (f32[1,128,2560]{2,1,0:T(8,128)S(1)}, f32[1,128,2560]{2,1,0:T(8,128)}, u32[]{:S(2)}) copy-start(f32[1,128,2560]{2,1,0:T(8,128)} %param.14) | copy-start | bytes 3932164
  9.5 523.1 %copy-start.2 = (bf16[1,128,2560]{2,1,0:T(8,128)(2,1)S(1)}, bf16[1,128,2560]{2,1,0:T(8,128)(2,1)}, u32[]{:S(2)}) copy-start(bf16[1,128,2560]{2,1,0:T(8,128)(2,1)} %param.13) | copy-start | bytes 1966084
  531.6 2.0 copy-start.3
  531.6 2.0 copy-start.4
  533.4 1.6 copy-start.9
  533.4 1.6 copy-start.10
  533.6 13.8 %copy-start.5 = (f32[128,20]{0,1:T(8,128)S(1)}, f32[128,20]{0,1:T(8,128)}, u32[]{:S(2)}) copy-start(f32[128,20]{0,1:T(8,128)} %param.20) | copy-start | bytes 30724
  533.6 13.9 %copy-start.6 = (f32[128,20]{0,1:T(8,128)S(1)}, f32[128,20]{0,1:T(8,128)}, u32[]{:S(2)}) copy-start(f32[128,20]{0,1:T(8,128)} %param.21) | copy-start | bytes 30724
  994.6 3.3 copy-start.7
  994.6 3.3 copy-start.8
Sparse Core Ops, SparseCore 0:
  535.1 458.2 all-reduce.3
where the time goes:
time: 1040 us
  blocking collectives  550 us (53%)
  waiting for transfers between devices  446 us (43%)
  between operations  15.8 us (2%)
  matrix products  12.1 us (1%)
    psum x1, blocking collectives, body(): lax.psum((project(key_basis, merged_key), project(router_basis, merged_ro...  497 us
    psum x1, waiting for transfers between devices, body(): lax.psum(jnp.concatenate([key_part, router_part], axis=1), ('dp', 'shard'))  446 us
  transfers between devices with their start and end apart: 1, of which 1 were waited for; matrix products, arithmetic and copies ran while one was open for 0% of the time, Pallas kernels for 0%

commit v1 on v0

--- a/solution.py
+++ b/solution.py
@@ -73,7 +73,7 @@
     router_part = lax.dot_general(
         merged_router, ortho_router, (((0,), (1,)), ((), ())), precision=highest
     )
-    column_sum = lax.psum(jnp.concatenate([key_part, router_part], axis=1), ("dp", "shard"))
+    column_sum = lax.psum(lax.psum(jnp.concatenate([key_part, router_part], axis=1), "shard"), "dp")
     columns = column_sum / replicas
     approx_key = lax.dot_general(
         ortho_key, columns[:, :rank_size], (((0,), (1,)), ((), ())), precision=highest

time: 1040 us -> 975 us (0.938)
  the two profiles are of different devices: /device:TPU:8 before, /device:TPU:2 now
where the time goes in v1:
time: 975 us
  blocking collectives  552 us (57%)
  waiting for transfers between devices  382 us (39%)
  between operations  15.9 us (2%)
  matrix products  12.1 us (1%)
    psum x1, blocking collectives, body(): lax.psum((project(key_basis, merged_key), project(router_basis, merged_ro...  502 us
    psum x1, waiting for transfers between devices, body(): lax.psum(lax.psum(jnp.concatenate([key_part, router_part], axis=1), 'shar...  330 us
    psum x1, waiting for transfers between devices, body(): lax.psum(jnp.concatenate([key_part, router_part], axis=1), 'shard')  52.4 us
  transfers between devices with their start and end apart: 2, of which 2 were waited for; matrix products, arithmetic and copies ran while one was open for 0% of the time, Pallas kernels for 0%

profile of v1, /device:TPU:2, one launch (start us, length us, event | category | flops | bytes accessed | tf_op | source)
XLA Modules:
  0.0 974.6 jit_solution(10453473724287904602)
XLA Ops:
  7.2 0.0 copy-start
  7.2 0.0 all-reduce.5.cloned.1.call-start
  7.2 0.7 bitcast_convert_fusion
  8.0 1.4 convolution_bitcast_fusion
  9.4 0.0 copy-done
  9.5 0.0 copy-start.2
  9.5 2.9 fusion.5
  12.4 502.2 %all-reduce = (f32[32,128]{1,0:T(8,128)S(1)}, f32[32,16]{0,1:T(8,128)S(1)}, f32[2,640]{1,0:T(2,128)S(1)}) all-reduce(f32[32,128]{1,0:T(8,128)S(1)} %fusion.5, f32[32,16]{0,1:T(8,128)S(1)} %convolution_bitcast_fusion, f32[2,640]{1,0:T(2,128)S(1)} %bitcast_convert_fusion), channel_id=1, replica_groups=mesh['dp'=128,'shard'=4] {'dp'}, use_global_device_ids=true, to_apply=%region_0.0 | all-reduce | flops 5888 | bytes 47104 | tf_op jit(solution)/shard_map/psum | solution.py:61
  514.6 0.1 fusion.31
  514.8 0.2 fusion.37
  515.0 14.1 %all-reduce.1 = (f32[32,32]{1,0:T(8,128)S(1)}, f32[32,32]{1,0:T(8,128)S(1)}) all-reduce(f32[32,32]{1,0:T(8,128)S(1)} %fusion.31, f32[32,32]{1,0:T(8,128)S(1)} %fusion.37), channel_id=1, replica_groups=mesh['dp'=128,'shard'=4] {'shard'}, use_global_device_ids=true, to_apply=%region_1.0 | all-reduce | flops 2048 | bytes 16384 | tf_op jit(solution)/shard_map/psum | solution.py:69
  529.1 0.6 multiply_reduce_fusion
  530.5 0.1 fusion.11
  530.6 0.1 fusion.27
  530.8 0.1 fusion.24
  530.9 0.2 fusion.10
  531.1 0.1 fusion.39
  531.2 0.1 fusion.38
  531.4 0.2 fusion.9
  531.5 0.1 fusion.40
  531.7 0.1 fusion.41
  532.6 0.1 fusion.15
  532.7 0.1 fusion.26
  532.9 0.1 fusion.25
  533.0 0.2 fusion.14
  533.2 0.1 fusion.33
  533.3 0.1 fusion.32
  533.4 0.2 fusion.13
  533.6 0.1 fusion.34
  533.8 0.0 copy-start.3
  533.8 0.1 fusion.35
  533.9 0.2 fusion.8
  534.1 0.1 fusion.42
  534.2 0.2 fusion.12
  534.4 0.1 fusion.36
  534.5 0.2 convolution_divide_fusion
  534.7 0.9 fusion
  535.6 0.1 convolution_divide_fusion.1
  535.7 0.0 copy-done.3
  535.8 0.5 fusion.20
  536.3 0.9 pad_maximum_fusion
  537.2 0.0 all-reduce.5.cloned.1.call-update
  537.2 0.0 all-reduce.7.cloned.1.call-start
  537.2 52.4 %all-reduce.5.cloned.1.call-done = f32[2560,64]{0,1:T(8,128)} async-done(((f32[2560,64]{0,1:T(8,128)}), f32[2560,64]{0,1:T(8,128)}) %all-reduce.5.cloned.1.call-update) | async-done | bytes 655376 | tf_op jit(solution)/shard_map/psum | solution.py:76
  589.7 0.0 all-reduce.7.cloned.1.call-update
  589.7 0.6 fusion.28
  590.3 11.5 %all_gather.11 = bf16[2,2560]{1,0:T(2,128)(2,1)S(1)} all-gather(bf16[2,640]{1,0:T(2,128)(2,1)S(1)} %get-tuple-element.27), channel_id=1, replica_groups=mesh['dp'=128,'shard'=4] {'shard'}, dimensions={1}, use_global_device_ids=true | all-gather | bytes 12800 | tf_op jit(solution)/shard_map/all_gather | solution.py:98
  601.8 0.1 copy.24
  601.9 0.1 copy.25
  602.0 329.7 %all-reduce.7.cloned.1.call-done = f32[2560,64]{0,1:T(8,128)} async-done(((f32[2560,64]{0,1:T(8,128)}), f32[2560,64]{0,1:T(8,128)}) %all-reduce.7.cloned.1.call-update) | async-done | bytes 655376 | tf_op jit(solution)/shard_map/psum | solution.py:76
  931.7 1.1 broadcast_multiply_fusion
  932.9 0.3 fusion.16
  933.2 2.3 fusion.18
  935.5 0.7 fusion.23
  936.2 0.7 fusion.29
  936.9 11.9 %all_gather.10 = bf16[64,20]{1,0:T(8,128)(2,1)S(1)} all-gather(bf16[16,20]{1,0:T(8,128)(2,1)S(1)} %get-tuple-element.30), channel_id=1, replica_groups=mesh['dp'=128,'shard'=4] {'shard'}, dimensions={0}, use_global_device_ids=true | all-gather | bytes 3200 | tf_op jit(solution)/shard_map/all_gather | solution.py:97
  948.8 0.7 copy.29
  949.5 2.6 fusion.4
  952.1 1.0 fusion.30
  953.1 0.7 copy.27
  953.7 0.7 copy.26
  954.4 12.0 %all_gather.9 = bf16[512,20]{1,0:T(8,128)(2,1)S(1)} all-gather(bf16[128,20]{1,0:T(8,128)(2,1)S(1)} %get-tuple-element.33), channel_id=1, replica_groups=mesh['dp'=128,'shard'=4] {'shard'}, dimensions={0}, use_global_device_ids=true | all-gather | bytes 25600 | tf_op jit(solution)/shard_map/all_gather | solution.py:96
  966.4 0.7 copy.28
  967.1 0.6 copy.33
  (17 shorter events, 0.1 us)
Async XLA Ops:
  7.2 2.3 copy-start
  7.2 582.5 %all-reduce.5.cloned.1.call-start = ((), (), s32[]{:S(2)}) async-start(), calls=%async_computation | async-start | bytes 1310720 | tf_op jit(solution)/shard_map/psum | solution.py:76
  9.4 525.2 %copy-start.1 = (f32[1,128,2560]{2,1,0:T(8,128)S(1)}, f32[1,128,2560]{2,1,0:T(8,128)}, u32[]{:S(2)}) copy-start(f32[1,128,2560]{2,1,0:T(8,128)} %param.14) | copy-start | bytes 3932164
  9.5 525.2 %copy-start.2 = (bf16[1,128,2560]{2,1,0:T(8,128)(2,1)S(1)}, bf16[1,128,2560]{2,1,0:T(8,128)(2,1)}, u32[]{:S(2)}) copy-start(bf16[1,128,2560]{2,1,0:T(8,128)(2,1)} %param.13) | copy-start | bytes 1966084
  533.8 2.0 copy-start.3
  533.8 2.0 copy-start.4
  536.2 53.5 %copy-start.9 = (f32[2,640]{1,0:T(2,128)S(1)}, f32[2,640]{1,0:T(2,128)}, u32[]{:S(2)}) copy-start(f32[2,640]{1,0:T(2,128)} %param.25) | copy-start | bytes 15364
  536.3 53.4 %copy-start.10 = (f32[2,640]{1,0:T(2,128)S(1)}, f32[2,640]{1,0:T(2,128)}, u32[]{:S(2)}) copy-start(f32[2,640]{1,0:T(2,128)} %param.24) | copy-start | bytes 15364
  536.3 65.5 %copy-start.5 = (f32[128,20]{0,1:T(8,128)S(1)}, f32[128,20]{0,1:T(8,128)}, u32[]{:S(2)}) copy-start(f32[128,20]{0,1:T(8,128)} %param.20) | copy-start | bytes 30724
  536.3 65.6 %copy-start.6 = (f32[128,20]{0,1:T(8,128)S(1)}, f32[128,20]{0,1:T(8,128)}, u32[]{:S(2)}) copy-start(f32[128,20]{0,1:T(8,128)} %param.21) | copy-start | bytes 30724
  537.2 394.6 %all-reduce.7.cloned.1.call-start = ((), (), s32[]{:S(2)}) async-start(), calls=%async_computation.1 | async-start | bytes 1310720 | tf_op jit(solution)/shard_map/psum | solution.py:76
  932.9 3.3 copy-start.7
  932.9 3.3 copy-start.8
Sparse Core Ops, SparseCore 0:
  537.3 52.2 all-reduce.4
  593.1 338.6 all-reduce.6
